TPU v7x, 32 devices: a whole 2x2x4 slice. The times are simulated.
32 devices in a mesh: area: 8 (over z, x), row: 4 (over y, core).
Axes of the slice: x: 2, y: 2, z: 4, core: 2. Of those that a mesh axis runs over, the one named last changes fastest.
Arguments:
- conductance_inverse: float32 [32, 1024, 1024], P(('area', 'row')), as said below
- cap_history: float32 [32, 1024, 128], P(('area', 'row')), may hold values from -3 to 3
- cap_conductance: float32 [32, 1024], P(('area', 'row')), may hold values from 0.5 to 0.8
- wave_history: float32 [32, 40, 32, 128], P(('area', 'row')), may hold values from -6 to 6
- line_partner: int32 [32, 32], P(('area', 'row')), may hold values from 0 to 31, as said below
- line_node: int32 [32, 32], P(('area', 'row')), may hold values from 0 to 1023
- line_delay: int32 [32, 32], P(('area', 'row')), may hold values from 20 to 40
- line_admittance: float32 [32, 32], P(('area', 'row')), may hold values from 0.2 to 1
- conv_node: int32 [32, 64], P(('area', 'row')), may hold values from 0 to 1023
- conv_count: int32 [32], P(('area', 'row')), may hold values from 1 to 64, as said below
- conv_state: float32 [32, 2, 64, 128], P(('area', 'row')), may hold values from -3 to 3
- conv_reference: float32 [32, 2, 64, 128], P(('area', 'row')), may hold values from -4 to 4
- conv_rate: float32 [32, 64], P(('area', 'row')), may hold values from 0.03 to 0.6
- conv_limit: float32 [32, 64], P(('area', 'row')), may hold values from 1 to 2.5
- port_node: int32 [32, 8], P(('area', 'row')), may hold values from 0 to 1023
- port_admittance: float32 [32, 8], P(('area', 'row')), may hold values from 0.3 to 1.2
- port_voltage_prev: float32 [2, 32, 8, 128], P(None, ('area', 'row')), may hold values from -5 to 5
- port_bus: int32 [32, 8], P('area'), may hold values from 0 to 20479
- transfer_impedance: float32 [2, 20480, 256], P(None, 'row', 'area'), may hold values from -0.75 to 0.75
Outputs:
- waves: float32 [32, 20, 32, 128], P(('area', 'row'))
- cap_history_out: float32 [32, 1024, 128], P(('area', 'row'))
- conv_state_out: float32 [32, 2, 64, 128], P(('area', 'row'))
- bus_voltage: float32 [2, 20480, 128], P(None, 'row')
- port_voltage: float32 [2, 32, 8, 128], P(None, ('area', 'row'))
Inputs may be any that keep to these rules, and one draw needn't show every extreme that they name: Slot l < 16 of subnetwork s and slot l + 16 of subnetwork (s + k_l) mod 32 are the two ends of one line, with k_l in 1 or 2 the same for every subnetwork and exactly 12 of the k_l equal to 1; so line_partner[s, l] = (s + k_l) mod 32 and line_partner[s, l + 16] = (s - k_l) mod 32. `conv_count`: some subnetwork has all 64 converters in service. `conductance_inverse`: each subnetwork's inverse nodal conductance matrix.
All inputs are finite; a program needn't handle non-finite values.
Results may differ from a plain program's by a relative error of at most 0.0003.
Values sent between devices are 32-bit elements; how exact they have to be, the bound alone decides.
A program may use at most 64 MiB of HBM per device.

v0:
```python
import math
import jax
import jax.numpy as jnp
from jax import lax
from jax.sharding import PartitionSpec as P

STEPS = 20
HIST = 40
NEAR = 12
HIGHEST = lax.Precision.HIGHEST
SAG_FACTOR = 0.3


def from_behind(x, axis, by):
    size = lax.axis_size(axis)
    return lax.ppermute(x, axis, [(i, (i + by) % size) for i in range(size)])


def window(
    ginv,
    start_hist,
    gcap,
    incoming,
    lnode,
    ladm,
    cnode,
    ccount,
    cstate,
    setpoint_flow,
    crate,
    climit,
    pnode,
    padm,
    pvolt,
):
    nodes = ginv.shape[0]
    lines = lnode.shape[0]
    convs = cnode.shape[0]
    index = jnp.concatenate([lnode, cnode, pnode])
    onehot = (jnp.arange(nodes, dtype=jnp.int32)[:, None] == index[None, :]).astype(jnp.float32)
    picker = onehot.T
    live = (jnp.arange(convs, dtype=jnp.int32) < ccount)[:, None]
    angles = jnp.arange(1, STEPS + 1, dtype=jnp.float32) * jnp.float32(2.0 * math.pi / STEPS)
    limit = climit[:, None]
    slew_limit = crate[:, None]

    def advance(carry, inputs):
        hist_now, inverter_axial_part, inverter_normal_part, acc_re, acc_im = carry
        inward, angle = inputs
        angle_cos_factor = jnp.cos(angle)
        angle_sin_factor = jnp.sin(angle)
        drive = jnp.where(
            live,
            inverter_axial_part * angle_cos_factor - inverter_normal_part * angle_sin_factor,
            0.0,
        )
        source = padm[:, None] * (pvolt[0] * angle_cos_factor - pvolt[1] * angle_sin_factor)
        stacked = jnp.concatenate([inward, drive, source], axis=0)
        right = hist_now + jnp.dot(onehot, stacked, precision=HIGHEST)
        volt = jnp.dot(ginv, right, precision=HIGHEST)
        probe = jnp.dot(picker, volt, precision=HIGHEST)
        at_line = probe[:lines]
        inverter_emf = probe[lines : lines + convs]
        at_port = probe[lines + convs :]
        outward = 2.0 * ladm[:, None] * at_line - inward
        flow = source - padm[:, None] * at_port
        acc_re = acc_re + flow * angle_cos_factor
        acc_im = acc_im - flow * angle_sin_factor
        unclipped_axial_part = (
            inverter_axial_part
            + slew_limit * (setpoint_flow[0] - inverter_axial_part)
            - SAG_FACTOR * inverter_emf * angle_cos_factor
        )
        unclipped_normal_part = (
            inverter_normal_part
            + slew_limit * (setpoint_flow[1] - inverter_normal_part)
            + SAG_FACTOR * inverter_emf * angle_sin_factor
        )
        inverter_axial_part = jnp.where(
            live, limit * jnp.tanh(unclipped_axial_part / limit), inverter_axial_part
        )
        inverter_normal_part = jnp.where(
            live, limit * jnp.tanh(unclipped_normal_part / limit), inverter_normal_part
        )
        hist_now = 2.0 * gcap[:, None] * volt - hist_now
        return ((hist_now, inverter_axial_part, inverter_normal_part, acc_re, acc_im), outward)

    zeros = jnp.zeros(pvolt.shape[1:], dtype=jnp.float32)
    carry = (start_hist, cstate[0], cstate[1], zeros, zeros)
    carry, outward = lax.scan(advance, carry, (incoming, angles))
    hist_end, inverter_axial_part, inverter_normal_part, acc_re, acc_im = carry
    current = jnp.stack([acc_re, acc_im]) * jnp.float32(2.0 / STEPS)
    return (outward, hist_end, jnp.stack([inverter_axial_part, inverter_normal_part]), current)


def per_device(
    conductance_inverse,
    cap_history,
    cap_conductance,
    wave_history,
    line_partner,
    line_node,
    line_delay,
    line_admittance,
    conv_node,
    conv_count,
    conv_state,
    conv_reference,
    conv_rate,
    conv_limit,
    port_node,
    port_admittance,
    port_voltage_prev,
    port_bus,
    transfer_impedance,
):
    subnets = lax.axis_size(("area", "row"))
    own = lax.axis_index(("area", "row"))
    history = wave_history[0]
    lines = history.shape[1]
    partner = line_partner[0]
    offset = (partner - own) % subnets
    signed = jnp.where(offset > subnets // 2, offset - subnets, offset)
    remote = (jnp.arange(lines, dtype=jnp.int32) + lines // 2) % lines
    combined = jnp.zeros(history.shape, jnp.float32)
    for reach in (1, -1, 2, -2):
        count = NEAR if abs(reach) == 1 else lines // 2 - NEAR
        sending = signed == reach
        order = jnp.argsort(jnp.where(sending, 0, 1), stable=True)[:count]
        packed = jnp.take(history, order, axis=1)
        arrived = from_behind(packed, ("area", "row"), reach)
        rank = jnp.cumsum(sending.astype(jnp.int32)) - 1
        slot = jnp.clip(rank[remote], 0, count - 1)
        picked = jnp.take(arrived, slot, axis=1)
        combined = combined + jnp.where((signed == -reach)[None, :, None], picked, 0.0)
    delay = line_delay[0]
    where_now = jnp.arange(STEPS, dtype=jnp.int32)[:, None] - delay[None, :] + HIST
    select = (where_now[:, None, :] == jnp.arange(HIST, dtype=jnp.int32)[None, :, None]).astype(
        jnp.float32
    )
    incoming = jnp.einsum("thl,hlc->tlc", select, combined, precision=HIGHEST)
    outward, hist_end, conv_out, current = window(
        conductance_inverse[0],
        cap_history[0],
        cap_conductance[0],
        incoming,
        line_node[0],
        line_admittance[0],
        conv_node[0],
        conv_count[0],
        conv_state[0],
        conv_reference[0],
        conv_rate[0],
        conv_limit[0],
        port_node[0],
        port_admittance[0],
        port_voltage_prev[:, 0],
    )
    bus_rows = transfer_impedance.shape[1]
    cases = current.shape[2]
    piece = lax.all_gather(current[:, None], "row", axis=1, tiled=True)
    members = piece.shape[1]
    ports = piece.shape[2]
    flat = piece.reshape(2, members * ports, cases)
    real = jnp.dot(transfer_impedance[0], flat[0], precision=HIGHEST) - jnp.dot(
        transfer_impedance[1], flat[1], precision=HIGHEST
    )
    imag = jnp.dot(transfer_impedance[0], flat[1], precision=HIGHEST) + jnp.dot(
        transfer_impedance[1], flat[0], precision=HIGHEST
    )
    partial_bus = jnp.stack([real, imag])
    bus_voltage = lax.psum(partial_bus, "area")
    first_row = lax.axis_index("row") * bus_rows
    local_bus = (port_bus - first_row).reshape(-1)
    pick_rows = (local_bus[:, None] == jnp.arange(bus_rows, dtype=jnp.int32)[None, :]).astype(
        jnp.float32
    )
    gathered = jnp.einsum("jb,xbc->xjc", pick_rows, bus_voltage, precision=HIGHEST)
    gathered = gathered.reshape(2, port_bus.shape[0], port_bus.shape[1], cases)
    port_voltage = lax.psum_scatter(gathered, "row", scatter_dimension=1, tiled=True)
    return (outward[None], hist_end[None], conv_out[None], bus_voltage, port_voltage)


def solution(mesh):
    placed = (
        P(("area", "row"), None, None),
        P(("area", "row"), None, None),
        P(("area", "row"), None),
        P(("area", "row"), None, None, None),
        P(("area", "row"), None),
        P(("area", "row"), None),
        P(("area", "row"), None),
        P(("area", "row"), None),
        P(("area", "row"), None),
        P(("area", "row")),
        P(("area", "row"), None, None, None),
        P(("area", "row"), None, None, None),
        P(("area", "row"), None),
        P(("area", "row"), None),
        P(("area", "row"), None),
        P(("area", "row"), None),
        P(None, ("area", "row"), None, None),
        P("area", None),
        P(None, "row", "area"),
    )
    return jax.shard_map(
        per_device,
        mesh=mesh,
        in_specs=placed,
        out_specs=(
            P(("area", "row"), None, None, None),
            P(("area", "row"), None, None),
            P(("area", "row"), None, None, None),
            P(None, "row", None),
            P(None, ("area", "row"), None, None),
        ),
        check_vma=False,
    )
```

profile of v0, /device:TPU:0, one launch (start us, length us, event | category | flops | bytes accessed | tf_op | source)
XLA Modules:
  0.0 522.5 jit_solution(1617881758800676381)
XLA Ops:
  7.9 1.6 sort.61
  9.6 1.5 copy.56
  11.7 3.0 collective-permute-start.2
  14.7 1.6 sort.62
  17.0 4.0 collective-permute-start.3
  20.9 1.6 sort.60
  23.3 0.9 collective-permute-start.1
  24.2 1.6 sort.59
  32.1 3.7 collective-permute-done
  36.5 1.4 gather_fusion.7
  37.9 2.7 convolution_bitcast_fusion.2
  40.6 254.0 %while.23 = (s32[]{:T(128)}, f32[1024,128]{0,1:T(8,128)S(1)}, f32[64,128]{1,0:T(8,128)S(1)}, f32[64,128]{1,0:T(8,128)S(1)}, f32[8,128]{1,0:T(8,128)S(1)}, /*inde...) while((s32[]{:T(128)}, f32[1024,128]{0,1:T(8,128)S(1)}, ...), condition=%wide.region_9.14_spmd.clone.clone.clone, body=%wide.region_8.13_spmd.clone.clone.clone.sunk | while | flops 1938803712 | bytes 8437999 | solution.py:90
  43.4 0.9 constant_dynamic-slice_fusion.3
  45.1 6.7 %bitcast_subtract_fusion.4 = (f32[1024,128]{0,1:T(8,128)S(1)}, f32[128,1024]{1,0:T(8,128)S(1)}) fusion(f32[1024,128]{0,1:T(8,128)S(1)} %get-tuple-element.591, f32[1024]{0:T(1024)S(1)} %bitcast.217, f32[1024,128]{0,1:T(8,128)S(1)} %fusion.99, f32[1024,1024]{1,0:T(8,128)} %get-tuple-element.624), kind=kOutput, calls=%fused_computation.18.clone.1 | convolution fusion | flops 1610874880 | bytes 6295552 | tf_op jit(solution)/shard_map/while/body/eval_jaxpr/dot_general | solution.py:60
  56.1 0.9 constant_dynamic-slice_fusion.3
  57.8 6.7 %bitcast_subtract_fusion.4 = (f32[1024,128]{0,1:T(8,128)S(1)}, f32[128,1024]{1,0:T(8,128)S(1)}) fusion(f32[1024,128]{0,1:T(8,128)S(1)} %get-tuple-element.591, f32[1024]{0:T(1024)S(1)} %bitcast.217, f32[1024,128]{0,1:T(8,128)S(1)} %fusion.99, f32[1024,1024]{1,0:T(8,128)} %get-tuple-element.624), kind=kOutput, calls=%fused_computation.18.clone.1 | convolution fusion | flops 1610874880 | bytes 6295552 | tf_op jit(solution)/shard_map/while/body/eval_jaxpr/dot_general | solution.py:60
  68.8 0.9 constant_dynamic-slice_fusion.3
  70.5 6.7 %bitcast_subtract_fusion.4 = (f32[1024,128]{0,1:T(8,128)S(1)}, f32[128,1024]{1,0:T(8,128)S(1)}) fusion(f32[1024,128]{0,1:T(8,128)S(1)} %get-tuple-element.591, f32[1024]{0:T(1024)S(1)} %bitcast.217, f32[1024,128]{0,1:T(8,128)S(1)} %fusion.99, f32[1024,1024]{1,0:T(8,128)} %get-tuple-element.624), kind=kOutput, calls=%fused_computation.18.clone.1 | convolution fusion | flops 1610874880 | bytes 6295552 | tf_op jit(solution)/shard_map/while/body/eval_jaxpr/dot_general | solution.py:60
  81.5 0.9 constant_dynamic-slice_fusion.3
  83.2 6.7 %bitcast_subtract_fusion.4 = (f32[1024,128]{0,1:T(8,128)S(1)}, f32[128,1024]{1,0:T(8,128)S(1)}) fusion(f32[1024,128]{0,1:T(8,128)S(1)} %get-tuple-element.591, f32[1024]{0:T(1024)S(1)} %bitcast.217, f32[1024,128]{0,1:T(8,128)S(1)} %fusion.99, f32[1024,1024]{1,0:T(8,128)} %get-tuple-element.624), kind=kOutput, calls=%fused_computation.18.clone.1 | convolution fusion | flops 1610874880 | bytes 6295552 | tf_op jit(solution)/shard_map/while/body/eval_jaxpr/dot_general | solution.py:60
  94.2 0.9 constant_dynamic-slice_fusion.3
  95.9 6.7 %bitcast_subtract_fusion.4 = (f32[1024,128]{0,1:T(8,128)S(1)}, f32[128,1024]{1,0:T(8,128)S(1)}) fusion(f32[1024,128]{0,1:T(8,128)S(1)} %get-tuple-element.591, f32[1024]{0:T(1024)S(1)} %bitcast.217, f32[1024,128]{0,1:T(8,128)S(1)} %fusion.99, f32[1024,1024]{1,0:T(8,128)} %get-tuple-element.624), kind=kOutput, calls=%fused_computation.18.clone.1 | convolution fusion | flops 1610874880 | bytes 6295552 | tf_op jit(solution)/shard_map/while/body/eval_jaxpr/dot_general | solution.py:60
  106.9 0.9 constant_dynamic-slice_fusion.3
  108.6 6.7 %bitcast_subtract_fusion.4 = (f32[1024,128]{0,1:T(8,128)S(1)}, f32[128,1024]{1,0:T(8,128)S(1)}) fusion(f32[1024,128]{0,1:T(8,128)S(1)} %get-tuple-element.591, f32[1024]{0:T(1024)S(1)} %bitcast.217, f32[1024,128]{0,1:T(8,128)S(1)} %fusion.99, f32[1024,1024]{1,0:T(8,128)} %get-tuple-element.624), kind=kOutput, calls=%fused_computation.18.clone.1 | convolution fusion | flops 1610874880 | bytes 6295552 | tf_op jit(solution)/shard_map/while/body/eval_jaxpr/dot_general | solution.py:60
  119.6 0.9 constant_dynamic-slice_fusion.3
  121.3 6.7 %bitcast_subtract_fusion.4 = (f32[1024,128]{0,1:T(8,128)S(1)}, f32[128,1024]{1,0:T(8,128)S(1)}) fusion(f32[1024,128]{0,1:T(8,128)S(1)} %get-tuple-element.591, f32[1024]{0:T(1024)S(1)} %bitcast.217, f32[1024,128]{0,1:T(8,128)S(1)} %fusion.99, f32[1024,1024]{1,0:T(8,128)} %get-tuple-element.624), kind=kOutput, calls=%fused_computation.18.clone.1 | convolution fusion | flops 1610874880 | bytes 6295552 | tf_op jit(solution)/shard_map/while/body/eval_jaxpr/dot_general | solution.py:60
  132.3 0.9 constant_dynamic-slice_fusion.3
  134.0 6.7 %bitcast_subtract_fusion.4 = (f32[1024,128]{0,1:T(8,128)S(1)}, f32[128,1024]{1,0:T(8,128)S(1)}) fusion(f32[1024,128]{0,1:T(8,128)S(1)} %get-tuple-element.591, f32[1024]{0:T(1024)S(1)} %bitcast.217, f32[1024,128]{0,1:T(8,128)S(1)} %fusion.99, f32[1024,1024]{1,0:T(8,128)} %get-tuple-element.624), kind=kOutput, calls=%fused_computation.18.clone.1 | convolution fusion | flops 1610874880 | bytes 6295552 | tf_op jit(solution)/shard_map/while/body/eval_jaxpr/dot_general | solution.py:60
  145.0 0.9 constant_dynamic-slice_fusion.3
  146.7 6.7 %bitcast_subtract_fusion.4 = (f32[1024,128]{0,1:T(8,128)S(1)}, f32[128,1024]{1,0:T(8,128)S(1)}) fusion(f32[1024,128]{0,1:T(8,128)S(1)} %get-tuple-element.591, f32[1024]{0:T(1024)S(1)} %bitcast.217, f32[1024,128]{0,1:T(8,128)S(1)} %fusion.99, f32[1024,1024]{1,0:T(8,128)} %get-tuple-element.624), kind=kOutput, calls=%fused_computation.18.clone.1 | convolution fusion | flops 1610874880 | bytes 6295552 | tf_op jit(solution)/shard_map/while/body/eval_jaxpr/dot_general | solution.py:60
  157.7 0.9 constant_dynamic-slice_fusion.3
  159.4 6.7 %bitcast_subtract_fusion.4 = (f32[1024,128]{0,1:T(8,128)S(1)}, f32[128,1024]{1,0:T(8,128)S(1)}) fusion(f32[1024,128]{0,1:T(8,128)S(1)} %get-tuple-element.591, f32[1024]{0:T(1024)S(1)} %bitcast.217, f32[1024,128]{0,1:T(8,128)S(1)} %fusion.99, f32[1024,1024]{1,0:T(8,128)} %get-tuple-element.624), kind=kOutput, calls=%fused_computation.18.clone.1 | convolution fusion | flops 1610874880 | bytes 6295552 | tf_op jit(solution)/shard_map/while/body/eval_jaxpr/dot_general | solution.py:60
  170.4 0.9 constant_dynamic-slice_fusion.3
  172.1 6.7 %bitcast_subtract_fusion.4 = (f32[1024,128]{0,1:T(8,128)S(1)}, f32[128,1024]{1,0:T(8,128)S(1)}) fusion(f32[1024,128]{0,1:T(8,128)S(1)} %get-tuple-element.591, f32[1024]{0:T(1024)S(1)} %bitcast.217, f32[1024,128]{0,1:T(8,128)S(1)} %fusion.99, f32[1024,1024]{1,0:T(8,128)} %get-tuple-element.624), kind=kOutput, calls=%fused_computation.18.clone.1 | convolution fusion | flops 1610874880 | bytes 6295552 | tf_op jit(solution)/shard_map/while/body/eval_jaxpr/dot_general | solution.py:60
  183.1 0.9 constant_dynamic-slice_fusion.3
  184.8 6.7 %bitcast_subtract_fusion.4 = (f32[1024,128]{0,1:T(8,128)S(1)}, f32[128,1024]{1,0:T(8,128)S(1)}) fusion(f32[1024,128]{0,1:T(8,128)S(1)} %get-tuple-element.591, f32[1024]{0:T(1024)S(1)} %bitcast.217, f32[1024,128]{0,1:T(8,128)S(1)} %fusion.99, f32[1024,1024]{1,0:T(8,128)} %get-tuple-element.624), kind=kOutput, calls=%fused_computation.18.clone.1 | convolution fusion | flops 1610874880 | bytes 6295552 | tf_op jit(solution)/shard_map/while/body/eval_jaxpr/dot_general | solution.py:60
  195.8 0.9 constant_dynamic-slice_fusion.3
  197.5 6.7 %bitcast_subtract_fusion.4 = (f32[1024,128]{0,1:T(8,128)S(1)}, f32[128,1024]{1,0:T(8,128)S(1)}) fusion(f32[1024,128]{0,1:T(8,128)S(1)} %get-tuple-element.591, f32[1024]{0:T(1024)S(1)} %bitcast.217, f32[1024,128]{0,1:T(8,128)S(1)} %fusion.99, f32[1024,1024]{1,0:T(8,128)} %get-tuple-element.624), kind=kOutput, calls=%fused_computation.18.clone.1 | convolution fusion | flops 1610874880 | bytes 6295552 | tf_op jit(solution)/shard_map/while/body/eval_jaxpr/dot_general | solution.py:60
  208.5 0.9 constant_dynamic-slice_fusion.3
  210.2 6.7 %bitcast_subtract_fusion.4 = (f32[1024,128]{0,1:T(8,128)S(1)}, f32[128,1024]{1,0:T(8,128)S(1)}) fusion(f32[1024,128]{0,1:T(8,128)S(1)} %get-tuple-element.591, f32[1024]{0:T(1024)S(1)} %bitcast.217, f32[1024,128]{0,1:T(8,128)S(1)} %fusion.99, f32[1024,1024]{1,0:T(8,128)} %get-tuple-element.624), kind=kOutput, calls=%fused_computation.18.clone.1 | convolution fusion | flops 1610874880 | bytes 6295552 | tf_op jit(solution)/shard_map/while/body/eval_jaxpr/dot_general | solution.py:60
  221.2 0.9 constant_dynamic-slice_fusion.3
  222.9 6.7 %bitcast_subtract_fusion.4 = (f32[1024,128]{0,1:T(8,128)S(1)}, f32[128,1024]{1,0:T(8,128)S(1)}) fusion(f32[1024,128]{0,1:T(8,128)S(1)} %get-tuple-element.591, f32[1024]{0:T(1024)S(1)} %bitcast.217, f32[1024,128]{0,1:T(8,128)S(1)} %fusion.99, f32[1024,1024]{1,0:T(8,128)} %get-tuple-element.624), kind=kOutput, calls=%fused_computation.18.clone.1 | convolution fusion | flops 1610874880 | bytes 6295552 | tf_op jit(solution)/shard_map/while/body/eval_jaxpr/dot_general | solution.py:60
  233.9 0.9 constant_dynamic-slice_fusion.3
  235.6 6.7 %bitcast_subtract_fusion.4 = (f32[1024,128]{0,1:T(8,128)S(1)}, f32[128,1024]{1,0:T(8,128)S(1)}) fusion(f32[1024,128]{0,1:T(8,128)S(1)} %get-tuple-element.591, f32[1024]{0:T(1024)S(1)} %bitcast.217, f32[1024,128]{0,1:T(8,128)S(1)} %fusion.99, f32[1024,1024]{1,0:T(8,128)} %get-tuple-element.624), kind=kOutput, calls=%fused_computation.18.clone.1 | convolution fusion | flops 1610874880 | bytes 6295552 | tf_op jit(solution)/shard_map/while/body/eval_jaxpr/dot_general | solution.py:60
  246.6 0.9 constant_dynamic-slice_fusion.3
  248.3 6.7 %bitcast_subtract_fusion.4 = (f32[1024,128]{0,1:T(8,128)S(1)}, f32[128,1024]{1,0:T(8,128)S(1)}) fusion(f32[1024,128]{0,1:T(8,128)S(1)} %get-tuple-element.591, f32[1024]{0:T(1024)S(1)} %bitcast.217, f32[1024,128]{0,1:T(8,128)S(1)} %fusion.99, f32[1024,1024]{1,0:T(8,128)} %get-tuple-element.624), kind=kOutput, calls=%fused_computation.18.clone.1 | convolution fusion | flops 1610874880 | bytes 6295552 | tf_op jit(solution)/shard_map/while/body/eval_jaxpr/dot_general | solution.py:60
  259.3 0.9 constant_dynamic-slice_fusion.3
  261.0 6.7 %bitcast_subtract_fusion.4 = (f32[1024,128]{0,1:T(8,128)S(1)}, f32[128,1024]{1,0:T(8,128)S(1)}) fusion(f32[1024,128]{0,1:T(8,128)S(1)} %get-tuple-element.591, f32[1024]{0:T(1024)S(1)} %bitcast.217, f32[1024,128]{0,1:T(8,128)S(1)} %fusion.99, f32[1024,1024]{1,0:T(8,128)} %get-tuple-element.624), kind=kOutput, calls=%fused_computation.18.clone.1 | convolution fusion | flops 1610874880 | bytes 6295552 | tf_op jit(solution)/shard_map/while/body/eval_jaxpr/dot_general | solution.py:60
  272.0 0.9 constant_dynamic-slice_fusion.3
  273.7 6.7 %bitcast_subtract_fusion.4 = (f32[1024,128]{0,1:T(8,128)S(1)}, f32[128,1024]{1,0:T(8,128)S(1)}) fusion(f32[1024,128]{0,1:T(8,128)S(1)} %get-tuple-element.591, f32[1024]{0:T(1024)S(1)} %bitcast.217, f32[1024,128]{0,1:T(8,128)S(1)} %fusion.99, f32[1024,1024]{1,0:T(8,128)} %get-tuple-element.624), kind=kOutput, calls=%fused_computation.18.clone.1 | convolution fusion | flops 1610874880 | bytes 6295552 | tf_op jit(solution)/shard_map/while/body/eval_jaxpr/dot_general | solution.py:60
  284.7 0.9 constant_dynamic-slice_fusion.3
  286.4 6.7 %bitcast_subtract_fusion.4 = (f32[1024,128]{0,1:T(8,128)S(1)}, f32[128,1024]{1,0:T(8,128)S(1)}) fusion(f32[1024,128]{0,1:T(8,128)S(1)} %get-tuple-element.591, f32[1024]{0:T(1024)S(1)} %bitcast.217, f32[1024,128]{0,1:T(8,128)S(1)} %fusion.99, f32[1024,1024]{1,0:T(8,128)} %get-tuple-element.624), kind=kOutput, calls=%fused_computation.18.clone.1 | convolution fusion | flops 1610874880 | bytes 6295552 | tf_op jit(solution)/shard_map/while/body/eval_jaxpr/dot_general | solution.py:60
  294.6 5.4 %all_gather.3 = f32[2,4,8,128]{3,2,1,0:T(8,128)S(1)} all-gather(f32[2,1,8,128]{3,2,1,0:T(8,128)S(1)} %maximum_multiply_fusion), channel_id=1, replica_groups=mesh['area'=8,'row'=4] {'row'}, dimensions={1}, use_global_device_ids=true | all-gather | bytes 40960 | tf_op jit(solution)/shard_map/all_gather | solution.py:161
  300.0 2.2 fusion.39
  302.2 2.2 fusion.41
  304.5 2.3 fusion.36
  306.8 2.3 fusion.35
  309.0 2.9 pad_maximum_fusion
  313.4 1.0 copy.48
  315.0 177.5 %all-reduce.3.cloned.1.call-done = f32[2,5120,128]{1,2,0:T(8,128)} async-done(((f32[2,5120,128]{1,2,0:T(8,128)}), f32[2,5120,128]{1,2,0:T(8,128)}) %all-reduce.3.cloned.1.call-update) | async-done | bytes 5242896 | tf_op jit(solution)/shard_map/psum | solution.py:172
  492.5 5.2 convolution_bitcast_fusion.3
  497.7 10.9 %all-reduce = f32[2,4,8,128]{3,2,1,0:T(8,128)S(1)} all-reduce(f32[2,4,8,128]{3,2,1,0:T(8,128)S(1)} %convolution_bitcast_fusion.3), channel_id=2, replica_groups=mesh['area'=8,'row'=4] {'row'}, use_global_device_ids=true, to_apply=%region_11.16.clone | all-reduce | flops 8192 | bytes 65536
  508.6 1.2 constant_dynamic-slice_fusion.1
  509.8 5.9 %copy.50 = f32[2,5120,128]{2,1,0:T(8,128)} copy(f32[2,5120,128]{1,2,0:T(8,128)} %all-reduce.3.cloned.1.call-done) | data formatting | bytes 10485760
  (322 shorter events, 82.7 us)
Async XLA Ops:
  7.2 19.4 %copy-start.11 = (s32[1,32]{1,0:T(1,128)S(1)}, s32[1,32]{1,0:T(1,128)}, u32[]{:S(2)}) copy-start(s32[1,32]{1,0:T(1,128)} %param.33) | copy-start | bytes 388
  7.2 19.6 %copy-start.10 = (s32[1,32]{1,0:T(1,128)S(1)}, s32[1,32]{1,0:T(1,128)}, u32[]{:S(2)}) copy-start(s32[1,32]{1,0:T(1,128)} %param.35) | copy-start | bytes 388
  7.2 485.3 %all-reduce.3.cloned.1.call-start = ((), (), s32[]{:S(2)}) async-start(), calls=%async_computation | async-start | bytes 10485760 | tf_op jit(solution)/shard_map/psum | solution.py:172
  11.6 18.9 %copy-start.5 = (f32[1,2,64,128]{3,2,1,0:T(8,128)S(1)}, f32[1,2,64,128]{3,2,1,0:T(8,128)}, u32[]{:S(2)}) copy-start(f32[1,2,64,128]{3,2,1,0:T(8,128)} %param.39) | copy-start | bytes 196612
  11.7 19.8 %collective-permute-start.2 = (f32[40,4,128]{2,0,1:T(8,128)S(1)}, f32[40,4,128]{2,0,1:T(8,128)S(1)}, u32[]{:S(2)}, u32[]{:S(2)}) collective-permute-start(f32[40,4,128]{2,0,1:T(8,128)S(1)} %select_bitcast_fusion.3), channel_id=1, source_target_pairs={{0,2},{1,3},{2,4},{3,5},{4,6},{5,7},{6,8},{7,9},{8,10},{9,11},{10,... | collective-permute-start | bytes 245768 | tf_op jit(solution)/shard_map/ppermute | solution.py:16
  16.3 14.3 %copy-start.3 = (f32[1,1024,128]{2,1,0:T(8,128)S(1)}, f32[1,1024,128]{2,1,0:T(8,128)}, u32[]{:S(2)}) copy-start(f32[1,1024,128]{2,1,0:T(8,128)} %param.30) | copy-start | bytes 1572868
  17.0 13.9 %collective-permute-start.3 = (f32[40,4,128]{2,0,1:T(8,128)S(1)}, f32[40,4,128]{2,0,1:T(8,128)S(1)}, u32[]{:S(2)}, u32[]{:S(2)}) collective-permute-start(f32[40,4,128]{2,0,1:T(8,128)S(1)} %select_bitcast_fusion.2), channel_id=1, source_target_pairs={{0,30},{1,31},{2,0},{3,1},{4,2},{5,3},{6,4},{7,5},{8,6},{9,7},{10,... | collective-permute-start | bytes 245768 | tf_op jit(solution)/shard_map/ppermute | solution.py:16
  23.1 7.7 %copy-start.12 = (s32[1,8]{1,0:T(1,128)S(1)}, s32[1,8]{1,0:T(1,128)}, u32[]{:S(2)}) copy-start(s32[1,8]{1,0:T(1,128)} %param.43) | copy-start | bytes 100
  23.1 7.7 %copy-start.13 = (s32[1,64]{1,0:T(1,128)S(1)}, s32[1,64]{1,0:T(1,128)}, u32[]{:S(2)}) copy-start(s32[1,64]{1,0:T(1,128)} %param.37) | copy-start | bytes 772
  23.2 7.6 %copy-start.14 = (s32[1,32]{1,0:T(1,128)S(1)}, s32[1,32]{1,0:T(1,128)}, u32[]{:S(2)}) copy-start(s32[1,32]{1,0:T(1,128)} %param.34) | copy-start | bytes 388
  23.3 13.2 %collective-permute-start.1 = (f32[40,12,128]{2,0,1:T(8,128)S(1)}, f32[40,12,128]{2,0,1:T(8,128)S(1)}, u32[]{:S(2)}, u32[]{:S(2)}) collective-permute-start(f32[40,12,128]{2,0,1:T(8,128)S(1)} %select_bitcast_fusion), channel_id=1, source_target_pairs={{0,31},{1,0},{2,1},{3,2},{4,3},{5,4},{6,5},{7,6},{8,7},{9,8},{10,9... | collective-permute-start | bytes 737288 | tf_op jit(solution)/shard_map/ppermute | solution.py:16
  26.5 9.3 %collective-permute-start = (f32[40,12,128]{2,0,1:T(8,128)S(1)}, f32[40,12,128]{2,0,1:T(8,128)S(1)}, u32[]{:S(2)}, u32[]{:S(2)}) collective-permute-start(f32[40,12,128]{2,0,1:T(8,128)S(1)} %select_bitcast_fusion.1), channel_id=1, source_target_pairs={{0,1},{1,2},{2,3},{3,4},{4,5},{5,6},{6,7},{7,8},{8,9},{9,10},{10,1... | collective-permute-start | bytes 737288 | tf_op jit(solution)/shard_map/ppermute | solution.py:16
  36.4 4.2 copy-start.1
  36.4 4.2 copy-start.2
  36.4 4.2 copy-start.4
  36.4 4.2 copy-start.6
  36.4 4.2 copy-start.7
  36.4 4.2 copy-start.8
  36.4 4.2 copy-start.15
  40.6 259.4 %copy-start = (f32[2,5120,32]{1,2,0:T(8,128)S(1)}, f32[2,5120,32]{1,2,0:T(8,128)}, u32[]{:S(2)}) copy-start(f32[2,5120,32]{1,2,0:T(8,128)} %param.47) | copy-start | bytes 3932164
  312.0 0.7 copy-start.9
  312.0 0.8 copy-start.16
Sparse Core Ops, SparseCore 0:
  312.1 180.2 all-reduce.2
where the time goes:
time: 525 us; the launch traced here: 523 us
  waiting for transfers between devices  181 us (34%)
  matrix products  178 us (34%)
  local copies, waits for them, and re-layouts  49.6 us (9%)
  other arithmetic  45.4 us (9%)
  loops' own time  29.9 us (6%)
  blocking collectives  16.3 us (3%)
  between operations  14.6 us (3%)
  starting transfers between devices  8.01 us (2%)
    psum x1, waiting for transfers between devices, per_device(): bus_voltage = lax.psum(partial_bus, 'area')  177 us
    dot_general x20, matrix products, advance(): volt = jnp.dot(ginv, right, precision=HIGHEST)  134 us
    dynamic_slice x40, local copies, waits for them, and re-layouts, window(): carry, outward = lax.scan(advance, carry, (incoming, angles))  30 us
    another operation x1, loops' own time, window(): carry, outward = lax.scan(advance, carry, (incoming, angles))  29.9 us
    dynamic_update_slice x20, other arithmetic, window(): carry, outward = lax.scan(advance, carry, (incoming, angles))  13.7 us
    dot_general x20, matrix products, advance(): probe = jnp.dot(picker, volt, precision=HIGHEST)  13.4 us
    broadcast_in_dim x20, other arithmetic, advance(): jnp.where(live, inverter_axial_part * angle_cos_factor - inverter_normal_...  13.1 us
    dot_general x20, matrix products, advance(): right = hist_now + jnp.dot(onehot, stacked, precision=HIGHEST)  12.9 us
  transfers between devices with their start and end apart: 5, of which 2 were waited for; matrix products, arithmetic and copies ran while one was open for 3% of the time, Pallas kernels for 0%

commit v1 on v0

--- a/solution.py
+++ b/solution.py
@@ -169,7 +169,7 @@
         transfer_impedance[1], flat[0], precision=HIGHEST
     )
     partial_bus = jnp.stack([real, imag])
-    bus_voltage = lax.psum(partial_bus, "area")
+    bus_voltage = jnp.sum(lax.all_gather(partial_bus, "area"), axis=0)
     first_row = lax.axis_index("row") * bus_rows
     local_bus = (port_bus - first_row).reshape(-1)
     pick_rows = (local_bus[:, None] == jnp.arange(bus_rows, dtype=jnp.int32)[None, :]).astype(

time: 525 us -> 1160 us (2.21)
  waiting for transfers between devices: 181 us -> 792 us
  other arithmetic: 45.4 us -> 63.2 us
    all_gather x0 -> x1, waiting for transfers between devices: none -> 789 us  [per_device(): bus_voltage = jnp.sum(lax.all_gather(partial_bus, 'area'), axis=0)]
    psum x1 -> x0, waiting for transfers between devices: 177 us -> none  [per_device(): bus_voltage = lax.psum(partial_bus, 'area')]
    unnamed x2 -> x3, other arithmetic: 0.01 us -> 17.1 us
  transfers between devices with their start and end apart: 5 -> 5, of which waited for: 2 -> 2; matrix products, arithmetic and copies ran while one was open for 3% -> 1% of each run, Pallas kernels for 0% -> 0%
where the time goes in v1:
time: 1160 us; the launch traced here: 1150 us
  waiting for transfers between devices  792 us (68%)
  matrix products  177 us (15%)
  other arithmetic  63.2 us (5%)
  local copies, waits for them, and re-layouts  49.7 us (4%)
  loops' own time  30 us (3%)
  blocking collectives  16.3 us (1%)
  between operations  14.5 us (1%)
    all_gather x1, waiting for transfers between devices, per_device(): bus_voltage = jnp.sum(lax.all_gather(partial_bus, 'area'), axis=0)  789 us
    dot_general x20, matrix products, advance(): volt = jnp.dot(ginv, right, precision=HIGHEST)  134 us
    dynamic_slice x40, local copies, waits for them, and re-layouts, window(): carry, outward = lax.scan(advance, carry, (incoming, angles))  30 us
    another operation x1, loops' own time, window(): carry, outward = lax.scan(advance, carry, (incoming, angles))  30 us
  transfers between devices with their start and end apart: 5, of which 2 were waited for; matrix products, arithmetic and copies ran while one was open for 1% of the time, Pallas kernels for 0%

profile of v1, /device:TPU:0, one launch (start us, length us, event | category | flops | bytes accessed | tf_op | source)
XLA Modules:
  0.0 1154.4 jit_solution(5795788118191857820)
XLA Ops:
  7.2 1.5 copy.55
  9.4 1.6 sort.62
  11.7 7.0 collective-permute-start.3
  18.6 1.6 sort.61
  20.9 1.6 sort.60
  23.3 4.5 collective-permute-start.1
  27.8 1.6 sort.59
  37.0 3.2 collective-permute-done
  40.2 1.4 gather_fusion.5
  41.6 2.7 convolution_bitcast_fusion.2
  44.4 254.0 %while.23 = (s32[]{:T(128)}, f32[1024,128]{0,1:T(8,128)S(1)}, f32[64,128]{1,0:T(8,128)S(1)}, f32[64,128]{1,0:T(8,128)S(1)}, f32[8,128]{1,0:T(8,128)S(1)}, /*inde...) while((s32[]{:T(128)}, f32[1024,128]{0,1:T(8,128)S(1)}, ...), condition=%wide.region_9.14_spmd.clone.clone.clone, body=%wide.region_8.13_spmd.clone.clone.clone.sunk | while | flops 1938803712 | bytes 8437999 | solution.py:90
  47.3 0.9 constant_dynamic-slice_fusion.3
  48.8 6.7 bitcast_subtract_fusion.4
  60.0 0.9 constant_dynamic-slice_fusion.3
  61.5 6.7 bitcast_subtract_fusion.4
  72.7 0.9 constant_dynamic-slice_fusion.3
  74.2 6.7 bitcast_subtract_fusion.4
  85.4 0.9 constant_dynamic-slice_fusion.3
  86.9 6.7 bitcast_subtract_fusion.4
  98.1 0.9 constant_dynamic-slice_fusion.3
  99.6 6.7 bitcast_subtract_fusion.4
  110.8 0.9 constant_dynamic-slice_fusion.3
  112.3 6.7 bitcast_subtract_fusion.4
  123.5 0.9 constant_dynamic-slice_fusion.3
  125.0 6.7 bitcast_subtract_fusion.4
  136.2 0.9 constant_dynamic-slice_fusion.3
  137.7 6.7 bitcast_subtract_fusion.4
  148.9 0.9 constant_dynamic-slice_fusion.3
  150.4 6.7 bitcast_subtract_fusion.4
  161.6 0.9 constant_dynamic-slice_fusion.3
  163.1 6.7 bitcast_subtract_fusion.4
  174.2 0.9 constant_dynamic-slice_fusion.3
  175.8 6.7 bitcast_subtract_fusion.4
  186.9 0.9 constant_dynamic-slice_fusion.3
  188.5 6.7 bitcast_subtract_fusion.4
  199.6 0.9 constant_dynamic-slice_fusion.3
  201.2 6.7 bitcast_subtract_fusion.4
  212.3 0.9 constant_dynamic-slice_fusion.3
  213.9 6.7 bitcast_subtract_fusion.4
  225.0 0.9 constant_dynamic-slice_fusion.3
  226.6 6.7 bitcast_subtract_fusion.4
  237.7 0.9 constant_dynamic-slice_fusion.3
  239.3 6.7 bitcast_subtract_fusion.4
  250.4 0.9 constant_dynamic-slice_fusion.3
  252.0 6.7 bitcast_subtract_fusion.4
  263.1 0.9 constant_dynamic-slice_fusion.3
  264.7 6.7 bitcast_subtract_fusion.4
  275.8 0.9 constant_dynamic-slice_fusion.3
  277.4 6.7 bitcast_subtract_fusion.4
  288.5 0.9 constant_dynamic-slice_fusion.3
  290.1 6.7 bitcast_subtract_fusion.4
  298.4 5.4 all_gather.9
  303.8 2.3 fusion.39
  306.0 2.2 fusion.41
  308.3 2.3 fusion.36
  310.5 2.3 fusion.35
  312.8 2.9 pad_maximum_fusion
  315.7 6.0 copy.45
  323.1 1.0 copy.44
  324.8 789.1 %all-gather.3.cloned.1.call-done = f32[16,5120,128]{2,1,0:T(8,128)} async-done(((f32[2,5120,128]{2,1,0:T(8,128)}), f32[16,5120,128]{2,1,0:T(8,128)}) %all-gather.3.cloned.1.call-update) | async-done | bytes 41943056 | tf_op jit(solution)/shard_map/all_gather | solution.py:172
  1113.8 17.1 %reduce_sum.9 = f32[2,5120,128]{2,1,0:T(8,128)} reduce(f32[8,2,5120,128]{3,2,1,0:T(8,128)} %bitcast.207, f32[]{:T(128)} %constant.83.clone.1), dimensions={0}, to_apply=%region_10.15 | reduce | flops 9175040 | bytes 47185924
  1130.9 4.5 convolution_bitcast_fusion.3
  1135.4 10.9 all-reduce
  1146.4 1.2 constant_dynamic-slice_fusion.1
  (323 shorter events, 83.3 us)
Async XLA Ops:
  7.2 23.6 %copy-start.11 = (s32[1,32]{1,0:T(1,128)S(1)}, s32[1,32]{1,0:T(1,128)}, u32[]{:S(2)}) copy-start(s32[1,32]{1,0:T(1,128)} %param.33) | copy-start | bytes 388
  7.2 23.7 %copy-start.5 = (f32[1,2,64,128]{3,2,1,0:T(8,128)S(1)}, f32[1,2,64,128]{3,2,1,0:T(8,128)}, u32[]{:S(2)}) copy-start(f32[1,2,64,128]{3,2,1,0:T(8,128)} %param.39) | copy-start | bytes 196612
  7.2 1106.6 %all-gather.3.cloned.1.call-start = ((), (), s32[]{:S(2)}) async-start(), calls=%async_computation | async-start | bytes 47185920 | tf_op jit(solution)/shard_map/all_gather | solution.py:172
  11.7 23.4 %collective-permute-start.3 = (f32[40,4,128]{2,0,1:T(8,128)S(1)}, f32[40,4,128]{2,0,1:T(8,128)S(1)}, u32[]{:S(2)}, u32[]{:S(2)}) collective-permute-start(f32[40,4,128]{2,0,1:T(8,128)S(1)} %select_bitcast_fusion.2), channel_id=1, source_target_pairs={{0,30},{1,31},{2,0},{3,1},{4,2},{5,3},{6,4},{7,5},{8,6},{9,7},{10,... | collective-permute-start | bytes 245768 | tf_op jit(solution)/shard_map/ppermute | solution.py:16
  20.3 14.4 %copy-start.10 = (s32[1,32]{1,0:T(1,128)S(1)}, s32[1,32]{1,0:T(1,128)}, u32[]{:S(2)}) copy-start(s32[1,32]{1,0:T(1,128)} %param.35) | copy-start | bytes 388
  20.3 14.5 %copy-start.3 = (f32[1,1024,128]{2,1,0:T(8,128)S(1)}, f32[1,1024,128]{2,1,0:T(8,128)}, u32[]{:S(2)}) copy-start(f32[1,1024,128]{2,1,0:T(8,128)} %param.30) | copy-start | bytes 1572868
  20.9 14.8 %collective-permute-start.2 = (f32[40,4,128]{2,0,1:T(8,128)S(1)}, f32[40,4,128]{2,0,1:T(8,128)S(1)}, u32[]{:S(2)}, u32[]{:S(2)}) collective-permute-start(f32[40,4,128]{2,0,1:T(8,128)S(1)} %select_bitcast_fusion.3), channel_id=1, source_target_pairs={{0,2},{1,3},{2,4},{3,5},{4,6},{5,7},{6,8},{7,9},{8,10},{9,11},{10,... | collective-permute-start | bytes 245768 | tf_op jit(solution)/shard_map/ppermute | solution.py:16
  23.1 11.8 %copy-start.12 = (s32[1,8]{1,0:T(1,128)S(1)}, s32[1,8]{1,0:T(1,128)}, u32[]{:S(2)}) copy-start(s32[1,8]{1,0:T(1,128)} %param.43) | copy-start | bytes 100
  23.1 11.8 %copy-start.13 = (s32[1,64]{1,0:T(1,128)S(1)}, s32[1,64]{1,0:T(1,128)}, u32[]{:S(2)}) copy-start(s32[1,64]{1,0:T(1,128)} %param.37) | copy-start | bytes 772
  23.2 11.8 %copy-start.14 = (s32[1,32]{1,0:T(1,128)S(1)}, s32[1,32]{1,0:T(1,128)}, u32[]{:S(2)}) copy-start(s32[1,32]{1,0:T(1,128)} %param.34) | copy-start | bytes 388
  23.3 13.0 %collective-permute-start.1 = (f32[40,12,128]{2,0,1:T(8,128)S(1)}, f32[40,12,128]{2,0,1:T(8,128)S(1)}, u32[]{:S(2)}, u32[]{:S(2)}) collective-permute-start(f32[40,12,128]{2,0,1:T(8,128)S(1)} %select_bitcast_fusion), channel_id=1, source_target_pairs={{0,31},{1,0},{2,1},{3,2},{4,3},{5,4},{6,5},{7,6},{8,7},{9,8},{10,9... | collective-permute-start | bytes 737288 | tf_op jit(solution)/shard_map/ppermute | solution.py:16
  30.8 9.4 collective-permute-start
  36.9 7.4 copy-start.1
  36.9 7.4 copy-start.2
  36.9 7.4 copy-start.4
  36.9 7.4 copy-start.6
  37.0 7.4 copy-start.7
  37.0 7.4 copy-start.8
  37.0 7.4 copy-start.15
  44.4 259.4 %copy-start = (f32[2,5120,32]{1,2,0:T(8,128)S(1)}, f32[2,5120,32]{1,2,0:T(8,128)}, u32[]{:S(2)}) copy-start(f32[2,5120,32]{1,2,0:T(8,128)} %param.47) | copy-start | bytes 3932164
  321.7 0.7 copy-start.9
  321.7 0.8 copy-start.16
Sparse Core Ops, SparseCore 0:
  321.9 791.9 all-gather.2
